TPU v7x, 32 devices: a whole 2x2x4 slice. The times are simulated.
32 devices in a mesh: st: 8 (over y, x, core), fq: 4 (over z).
Axes of the slice: x: 2, y: 2, z: 4, core: 2. Of those that a mesh axis runs over, the one named last changes fastest.
Arguments:
- signals: bfloat16 [512, 16384], P(('st', 'fq')), may hold values from -6 to 6
- freq_bins: int32 [1024], replicated, may hold values from 1 to 8191, as said below
- sensor_station: int32 [512], P('st'), may hold values from 0 to 255, as said below
- gain: bfloat16 [512, 768], P('st'), may hold values from -1.5 to 1.5
- damping: float32 [256, 768], P('st'), may hold values from 0 to 1
- damping_up: float32 [256, 768], P('st'), may hold values from 0 to 1
- phase_speed: float32 [768], replicated, may hold values from 0.5 to 4
Outputs:
- estimate: bfloat16 [256, 768, 1024], P(('st', 'fq'))
Inputs may be any that keep to these rules, and one draw needn't show every extreme that they name: `freq_bins`: distinct bin numbers. `sensor_station`: sensor s sits at one of the 32 stations starting at (s // 64) * 32.
All inputs are finite; a program needn't handle non-finite values.
Results may differ from a plain program's by a relative error of at most 0.015.
Values may be sent and summed in bfloat16 or wider, within the bound.
A program may use at most 320 MiB of HBM per device.

v0:
```python
import math
import jax
import jax.numpy as jnp
from jax import lax
from jax.sharding import PartitionSpec as P

NT = 16384
NF = 1024
TOUT = 1024


def shifted(block, axis, distance):
    devices = range(lax.axis_size(axis))
    route = [(i - distance, i) for i in devices if i - distance in devices]
    return lax.ppermute(block, axis, route)


def cmul(left, right):
    return jnp.stack(
        [left[0] * right[0] - left[1] * right[1], left[0] * right[1] + left[1] * right[0]]
    )


def phases(steps, freq_bins):
    angle = (steps[:, None] * freq_bins[None, :] % NT).astype(jnp.float32) * (2 * math.pi / NT)
    return (jnp.cos(angle), jnp.sin(angle))


def base_table(count, freq_bins):
    fine = min(count, 128)
    coarse = count // fine
    fine_cos, fine_sin = phases(lax.iota(jnp.int32, fine), freq_bins)
    big_cos, big_sin = phases(lax.iota(jnp.int32, coarse) * fine, freq_bins)
    table_cos = big_cos[:, None, :] * fine_cos[None] - big_sin[:, None, :] * fine_sin[None]
    table_sin = big_sin[:, None, :] * fine_cos[None] + big_cos[:, None, :] * fine_sin[None]
    return (table_cos.reshape(count, -1), table_sin.reshape(count, -1))


def phase_rotated(base_cos, base_sine_table, offset, freq_bins):
    row_cos, row_sin = phases(jnp.reshape(offset, (1,)).astype(jnp.int32), freq_bins)
    return (
        base_cos * row_cos - base_sine_table * row_sin,
        base_sine_table * row_cos + base_cos * row_sin,
    )


def on_device(signals, freq_bins, sensor_station, gain, damping, damping_up, phase_speed):
    sens_dev = signals.shape[0]
    width = min(NT, 2048)
    base_cos, base_sine_table = base_table(width, freq_bins)

    def add_block(index, total):
        start = index * width
        times = start + lax.iota(jnp.int32, width)
        hann = 0.5 - 0.5 * jnp.cos(times.astype(jnp.float32) * (2 * math.pi / NT))
        piece = lax.dynamic_slice_in_dim(signals, start, width, 1)
        windowed = (piece.astype(jnp.float32) * hann[None, :]).astype(jnp.bfloat16)
        turned_cos, shifted_imaginary_factor = phase_rotated(
            base_cos, base_sine_table, start, freq_bins
        )
        table = jnp.concatenate(
            [
                (turned_cos / math.sqrt(NT)).astype(jnp.bfloat16),
                (shifted_imaginary_factor / math.sqrt(NT)).astype(jnp.bfloat16),
            ],
            axis=1,
        )
        return total + jnp.dot(windowed, table, preferred_element_type=jnp.float32)

    spectra = lax.fori_loop(0, NT // width, add_block, jnp.zeros((sens_dev, 2 * NF), jnp.float32))
    spec_re = spectra[:, :NF].astype(jnp.bfloat16)
    spec_im = (-spectra[:, NF:]).astype(jnp.bfloat16)
    spec_re, spec_im = (
        lax.all_to_all(spec_re, "fq", split_axis=1, concat_axis=0, tiled=True),
        lax.all_to_all(spec_im, "fq", split_axis=1, concat_axis=0, tiled=True),
    )
    sens_block = spec_re.shape[0]
    freq_dev = spec_re.shape[1]
    width_state = gain.shape[1]
    st_dev = damping.shape[0]
    own_bins = lax.dynamic_slice_in_dim(freq_bins, lax.axis_index("fq") * freq_dev, freq_dev)
    theta = 2 * math.pi * (own_bins.astype(jnp.float32) / NT)[:, None] * phase_speed[None, :]
    rot_down = jnp.stack([jnp.cos(theta), -jnp.sin(theta)])
    rot_up = jnp.stack([jnp.cos(theta), jnp.sin(theta)])
    local = sensor_station - lax.axis_index("st") * st_dev
    onehot = (local[None, :] == lax.iota(jnp.int32, st_dev)[:, None]).astype(jnp.bfloat16)
    spec_own = jnp.stack([spec_re, spec_im]).transpose(0, 2, 1)
    selected = onehot[:, None, None, :] * spec_own[None]
    forcing = jnp.dot(selected.reshape(-1, sens_block), gain, preferred_element_type=jnp.float32)
    forcing = forcing.reshape(st_dev, 2, freq_dev, width_state)
    zeros = jnp.zeros((2, freq_dev, width_state), jnp.float32)
    identity = jnp.stack(
        [
            jnp.ones((freq_dev, width_state), jnp.float32),
            jnp.zeros((freq_dev, width_state), jnp.float32),
        ]
    )

    def march_down(carry, inputs):
        state, product = carry
        term, rate = inputs
        factor = rate[None, None, :] * rot_down
        state = cmul(factor, state) + term
        return ((state, cmul(factor, product)), state)

    (last_down, block_down), downstream_fields = lax.scan(
        march_down, (zeros, identity), (forcing, damping)
    )

    def march_upward(carry, inputs):
        state, product = carry
        term, rate, lower = inputs
        factor = rate[None, None, :] * rot_up
        state = cmul(factor, state) + term
        return ((state, cmul(factor, product)), state + lower)

    (first_up, block_up), partial_sum = lax.scan(
        march_upward, (zeros, identity), (forcing, damping_up, downstream_fields), reverse=True
    )

    def relay(turn, carry):
        from_below, from_above = carry
        output_downward = cmul(block_down, from_below) + last_down
        out_up = cmul(block_up, from_above) + first_up
        from_below = shifted(output_downward.astype(jnp.bfloat16), "st", 1).astype(
            output_downward.dtype
        )
        from_above = shifted(out_up.astype(jnp.bfloat16), "st", -1).astype(out_up.dtype)
        return (from_below, from_above)

    from_below, from_above = lax.fori_loop(0, lax.axis_size("st") - 1, relay, (zeros, zeros))

    def carry_down(state, rate):
        state = cmul(rate[None, None, :] * rot_down, state)
        return (state, state)

    ending_down, lifted_down = lax.scan(carry_down, from_below, damping)

    def carry_up(state, inputs):
        rate, base, lower = inputs
        state = cmul(rate[None, None, :] * rot_up, state)
        return (state, (base + lower + state).astype(jnp.bfloat16))

    ending_up, state_all = lax.scan(
        carry_up, from_above, (damping_up, partial_sum, lifted_down), reverse=True
    )
    out_cos, out_sin = base_table(TOUT, freq_bins)
    out_cos, out_sin = phase_rotated(out_cos, out_sin, NT - TOUT, freq_bins)
    inverse = jnp.stack(
        [
            (out_cos.T / math.sqrt(NF)).astype(jnp.bfloat16),
            (-out_sin.T / math.sqrt(NF)).astype(jnp.bfloat16),
        ]
    )
    return jnp.einsum(
        "kcfm,cft->kmt",
        lax.all_to_all(state_all, "fq", split_axis=0, concat_axis=2, tiled=True),
        inverse,
        preferred_element_type=jnp.float32,
    ).astype(jnp.bfloat16)


def solution(mesh):
    placed = (P(("st", "fq"), None), P(), P("st"), P("st", None), P("st", None), P("st", None), P())
    return jax.shard_map(
        on_device,
        mesh=mesh,
        in_specs=placed,
        out_specs=P(("st", "fq"), None, None),
        check_vma=False,
    )
```

profile of v0, /device:TPU:4, one launch (start us, length us, event | category | flops | bytes accessed | tf_op | source)
XLA Modules:
  0.0 2022.5 jit_solution(1297842721965463363)
XLA Ops:
  3.8 110.0 %while.98 = (s32[]{:T(128)}, f32[16,2048]{1,0:T(8,128)S(1)}, bf16[16,16384]{1,0:T(8,128)(2,1)}, s32[1024]{0:T(1024)}, f32[128,1024]{1,0:T(8,128)S(1)}, /*index=5...) while((s32[]{:T(128)}, f32[16,2048]{1,0:T(8,128)S(1)}, ...), condition=%wide.region_1.2_spmd.clone.clone.clone, body=%wide.region_0.1_spmd.clone.clone.clone.sunk | while | flops 184737792 | bytes 51876020 | solution.py:70
  7.0 5.8 fusion.92
  135.5 20.2 fusion.44
  155.7 16.3 broadcast.585.clone
  173.3 316.1 %while.95 = (s32[]{:T(128)}, f32[2,256,768]{2,1,0:T(8,128)}, f32[2,256,768]{2,1,0:T(8,128)}, f32[32,2,256,768]{3,2,1,0:T(8,128)}, f32[32,768]{1,0:T(8,128)}, /*i...) while((s32[]{:T(128)}, f32[2,256,768]{2,1,0:T(8,128)}, ...), condition=%wide.region_3.4_spmd.clone, body=%wide.region_2.3_spmd.clone.sunk | while | flops 5111811 | bytes 33040012 | solution.py:106
  489.4 16.2 broadcast.585.clone.1
  507.0 333.9 %while.96 = (s32[]{:T(128)}, f32[2,256,768]{2,1,0:T(8,128)}, f32[2,256,768]{2,1,0:T(8,128)}, f32[32,2,256,768]{3,2,1,0:T(8,128)}, f32[32,768]{1,0:T(8,128)}, /*i...) while((s32[]{:T(128)}, f32[2,256,768]{2,1,0:T(8,128)}, ...), condition=%wide.region_5.6_spmd.clone, body=%wide.region_4.5_spmd.clone.sunk | while | flops 5505028 | bytes 34612392 | solution.py:117
  841.0 217.8 %while.97 = (s32[]{:T(128)}, f32[2,256,768]{2,1,0:T(8,128)}, f32[2,256,768]{2,1,0:T(8,128)}, f32[2,256,768]{2,1,0:T(8,128)}, f32[2,256,768]{2,1,0:T(8,128)}, /*i...) while((s32[]{:T(128)}, f32[2,256,768]{2,1,0:T(8,128)}, ...), condition=%wide.region_7.8_spmd.clone, body=%wide.region_6.7_spmd.clone.sunk | while | flops 6291459 | bytes 66060612 | solution.py:131
  852.1 10.8 collective-permute-done.1
  882.8 11.7 collective-permute-done.1
  913.2 12.5 collective-permute-done.1
  944.5 12.8 collective-permute-done.1
  976.1 13.1 collective-permute-done.1
  1008.0 13.5 collective-permute-done.1
  1040.2 13.8 collective-permute-done.1
  1058.8 16.2 broadcast.585
  1075.0 137.9 %while.93 = (s32[]{:T(128)}, f32[2,256,768]{2,1,0:T(8,128)}, f32[32,2,256,768]{3,2,1,0:T(8,128)}, f32[32,768]{1,0:T(8,128)}, f32[2,256,768]{2,1,0:T(8,128)S(1)}, /*index=5*/s32[]{:T(128)}) while((s32[]{:T(128)}, f32[2,256,768]{2,1,0:T(8,128)}, f32[32,2,256,768]{3,2,1,0:T(8,128)}, f32[32,768]{1,0:T(8,128)}, f32[2,256,768]{2,1,0:T(8,128)S(1)}, ...), condition=%wide.region_9.10_spmd, body=%wide.region_8.9_spmd.sunk | while | flops 1966082 | bytes 18884196 | solution.py:137
  1212.9 8.8 broadcast_in_dim.20
  1221.7 138.6 %while.94 = (s32[]{:T(128)}, f32[2,256,768]{2,1,0:T(8,128)S(1)}, bf16[32,2,256,768]{3,2,1,0:T(8,128)(2,1)}, f32[32,768]{1,0:T(8,128)}, f32[2,256,768]{2,1,0:T(8,...) while((s32[]{:T(128)}, f32[2,256,768]{2,1,0:T(8,128)S(1)}, ...), condition=%wide.region_11.12_spmd, body=%wide.region_10.11_spmd.sunk | while | flops 3538947 | bytes 16524401 | solution.py:144
  1360.3 8.8 all-to-all-start.2
  1375.8 535.3 %all-to-all-done.2 = bf16[32,2,256,768]{3,2,1,0:T(8,128)(2,1)} async-done(((bf16[32,2,256,768]{3,2,1,0:T(8,128)(2,1)}), bf16[32,2,256,768]{3,2,1,0:T(8,128)(2,1)}, u32[]{:S(2)}, u32[]{:S(2)}) %all-to-all-start.2) | async-done | bytes 25165856 | tf_op jit(solution)/shard_map/all_to_all | solution.py:157
  1911.1 38.9 %copy.26 = bf16[4,8,2,256,768]{3,0,4,2,1:T(4,128)(2,1)} copy(bf16[4,8,2,256,768]{4,3,2,1,0:T(8,128)(2,1)} %bitcast.10) | data formatting | bytes 50331648 | tf_op jit(solution)/shard_map/all_to_all | solution.py:157
  1949.9 40.6 %all_to_all.46 = bf16[8,2,1024,768]{2,3,1,0:T(8,128)(2,1)} reshape(bf16[8,2,4,256,768]{3,2,4,1,0:T(4,128)(2,1)} %bitcast.140) | data formatting | bytes 50331648 | tf_op jit(solution)/shard_map/all_to_all | solution.py:157
  1990.5 32.0 %bitcast_convert_fusion = bf16[8,768,1024]{2,1,0:T(8,128)(2,1)} fusion(bf16[8,2,1024,768]{2,3,1,0:T(8,128)(2,1)} %all_to_all.46, bf16[1,1024,1024]{2,1,0:T(8,128)(2,1)} %get-tuple-element.875, bf16[1,1024,1024]{2,1,0:T(8,128)(2,1)S(1)} %get-tuple-element.874), kind=kOutput, calls=%fused_computation.80 | convolution fusion | flops 25778192384 | bytes 41943040 | tf_op jit(solution)/shard_map/kcfm,cft->kmt/dot_general | solution.py:155
  (1098 shorter events, 1190.6 us)
Async XLA Ops:
  0.0 135.5 %copy-start = (bf16[64,768]{1,0:T(8,128)(2,1)S(1)}, bf16[64,768]{1,0:T(8,128)(2,1)}, u32[]{:S(2)}) copy-start(bf16[64,768]{1,0:T(8,128)(2,1)} %param.22) | copy-start | bytes 294916
  3.8 116.3 %copy-start.16 = (f32[768]{0:T(1024)S(1)}, f32[768]{0:T(1024)}, u32[]{:S(2)}) copy-start(f32[768]{0:T(1024)} %param.25) | copy-start | bytes 9220
  113.8 16.0 copy-start.11
  113.8 16.0 copy-start.13
  113.8 10.3 copy-start.18
  114.5 10.5 all-to-all-start
  125.0 10.5 all-to-all-start.1
  155.7 16.3 copy-start.17
  846.7 16.2 collective-permute-start.1
  849.7 19.0 collective-permute-start
  877.3 17.1 collective-permute-start.1
  880.4 17.5 collective-permute-start
  906.5 19.2 collective-permute-start.1
  911.3 16.9 collective-permute-start
  936.8 20.6 %collective-permute-start.1 = (bf16[2,256,768]{2,1,0:T(8,128)(2,1)}, bf16[2,256,768]{2,1,0:T(8,128)(2,1)}, u32[]{:S(2)}, u32[]{:S(2)}) collective-permute-start(bf16[2,256,768]{2,1,0:T(8,128)(2,1)} %fusion.89), channel_id=1, source_target_pairs={{4,0},{8,4},{12,8},{16,12},{20,16},{24,20},{28,24},{5,1},{9,5},{13... | collective-permute-start | bytes 2359304 | tf_op jit(solution)/shard_map/while/body/eval_jaxpr/ppermute | solution.py:15
  942.6 17.2 collective-permute-start
  968.4 20.9 %collective-permute-start.1 = (bf16[2,256,768]{2,1,0:T(8,128)(2,1)}, bf16[2,256,768]{2,1,0:T(8,128)(2,1)}, u32[]{:S(2)}, u32[]{:S(2)}) collective-permute-start(bf16[2,256,768]{2,1,0:T(8,128)(2,1)} %fusion.89), channel_id=1, source_target_pairs={{4,0},{8,4},{12,8},{16,12},{20,16},{24,20},{28,24},{5,1},{9,5},{13... | collective-permute-start | bytes 2359304 | tf_op jit(solution)/shard_map/while/body/eval_jaxpr/ppermute | solution.py:15
  974.2 17.5 collective-permute-start
  1000.3 21.2 %collective-permute-start.1 = (bf16[2,256,768]{2,1,0:T(8,128)(2,1)}, bf16[2,256,768]{2,1,0:T(8,128)(2,1)}, u32[]{:S(2)}, u32[]{:S(2)}) collective-permute-start(bf16[2,256,768]{2,1,0:T(8,128)(2,1)} %fusion.89), channel_id=1, source_target_pairs={{4,0},{8,4},{12,8},{16,12},{20,16},{24,20},{28,24},{5,1},{9,5},{13... | collective-permute-start | bytes 2359304 | tf_op jit(solution)/shard_map/while/body/eval_jaxpr/ppermute | solution.py:15
  1006.1 17.8 collective-permute-start
  1032.5 21.5 %collective-permute-start.1 = (bf16[2,256,768]{2,1,0:T(8,128)(2,1)}, bf16[2,256,768]{2,1,0:T(8,128)(2,1)}, u32[]{:S(2)}, u32[]{:S(2)}) collective-permute-start(bf16[2,256,768]{2,1,0:T(8,128)(2,1)} %fusion.89), channel_id=1, source_target_pairs={{4,0},{8,4},{12,8},{16,12},{20,16},{24,20},{28,24},{5,1},{9,5},{13... | collective-permute-start | bytes 2359304 | tf_op jit(solution)/shard_map/while/body/eval_jaxpr/ppermute | solution.py:15
  1038.3 18.1 collective-permute-start
  1360.3 550.7 %all-to-all-start.2 = ((bf16[32,2,256,768]{3,2,1,0:T(8,128)(2,1)}), bf16[32,2,256,768]{3,2,1,0:T(8,128)(2,1)}, u32[]{:S(2)}, u32[]{:S(2)}) async-start(bf16[32,2,256,768]{3,2,1,0:T(8,128)(2,1)} %get-tuple-element.577), calls=%async_computation.2 | async-start | bytes 50331648 | tf_op jit(solution)/shard_map/all_to_all | solution.py:157
  1990.5 32.0 %copy-start.1 = (bf16[64,768]{1,0:T(8,128)(2,1)S(1)}, bf16[64,768]{1,0:T(8,128)(2,1)}, u32[]{:S(2)}) copy-start(bf16[64,768]{1,0:T(8,128)(2,1)} %param.22) | copy-start | bytes 294916
  (135 other events, 271.2 us)
where the time goes:
time: 2040 us; the launch traced here: 2020 us
  other arithmetic  925 us (45%)
  waiting for transfers between devices  632 us (31%)
  local copies, waits for them, and re-layouts  312 us (15%)
  matrix products  89.8 us (4%)
  starting transfers between devices  59.2 us (3%)
    all_to_all x1, waiting for transfers between devices, on_device(): lax.all_to_all(state_all, 'fq', split_axis=0, concat_axis=2, tiled=True)  535 us
    dynamic_update_slice x96, other arithmetic, on_device(): lax.scan(march_down, (zeros, identity), (forcing, damping))  259 us
    while x78, other arithmetic  119 us
    dynamic_update_slice x32, other arithmetic, on_device(): lax.scan(carry_up, from_above, (damping_up, partial_sum, lifted_down), re...  100 us
    dynamic_slice x128, local copies, waits for them, and re-layouts, on_device(): lax.scan(march_down, (zeros, identity), (forcing, damping))  96.4 us
    ppermute x14, waiting for transfers between devices, shifted(): return lax.ppermute(block, axis, route)  92.6 us
    add x32, other arithmetic, march_upward(): state = cmul(factor, state) + term  89.2 us
    add x32, other arithmetic, march_down(): state = cmul(factor, state) + term  88.3 us
  transfers between devices with their start and end apart: 17, of which 12 were waited for; matrix products, arithmetic and copies ran while one was open for 2% of the time, Pallas kernels for 0%

commit v1 on v0

--- a/solution.py
+++ b/solution.py
@@ -154,7 +154,12 @@
     )
     return jnp.einsum(
         "kcfm,cft->kmt",
-        lax.all_to_all(state_all, "fq", split_axis=0, concat_axis=2, tiled=True),
+        jnp.concatenate(
+            lax.all_to_all(
+                jnp.stack(jnp.split(state_all, lax.axis_size("fq"), axis=0)), "fq", 0, 0
+            ),
+            axis=2,
+        ),
         inverse,
         preferred_element_type=jnp.float32,
     ).astype(jnp.bfloat16)

time: 2040 us -> 2040 us (level)
    all_to_all x2 -> x0, local copies, waits for them, and re-layouts: 79.4 us -> none  [on_device(): lax.all_to_all(state_all, 'fq', split_axis=0, concat_axis=2, tiled=True)]
    reshape x0 -> x2, local copies, waits for them, and re-layouts: none -> 79.4 us  [on_device(): jnp.concatenate(lax.all_to_all(jnp.stack(jnp.split(state_all, lax.axis_si...]
    while x262, local copies, waits for them, and re-layouts: 73.4 us -> 43.8 us
    another operation x3 -> x4, local copies, waits for them, and re-layouts: 48.8 us -> 61.3 us
where the time goes in v1:
time: 2040 us; the launch traced here: 2020 us
  other arithmetic  938 us (46%)
  waiting for transfers between devices  632 us (31%)
  local copies, waits for them, and re-layouts  298 us (15%)
  matrix products  89.7 us (4%)
  starting transfers between devices  59.1 us (3%)
    all_to_all x1, waiting for transfers between devices, on_device(): lax.all_to_all(jnp.stack(jnp.split(state_all, lax.axis_size('fq'), axis=0...  536 us
    dynamic_update_slice x96, other arithmetic, on_device(): lax.scan(march_down, (zeros, identity), (forcing, damping))  259 us
    while x78, other arithmetic  119 us
    dynamic_slice x128, local copies, waits for them, and re-layouts, on_device(): lax.scan(march_down, (zeros, identity), (forcing, damping))  100 us
    dynamic_update_slice x32, other arithmetic, on_device(): lax.scan(carry_up, from_above, (damping_up, partial_sum, lifted_down), re...  100 us
    ppermute x14, waiting for transfers between devices, shifted(): return lax.ppermute(block, axis, route)  92.6 us
    add x32, other arithmetic, march_upward(): state = cmul(factor, state) + term  89.1 us
    add x32, other arithmetic, march_down(): state = cmul(factor, state) + term  88.1 us
  transfers between devices with their start and end apart: 17, of which 12 were waited for; matrix products, arithmetic and copies ran while one was open for 2% of the time, Pallas kernels for 0%

profile of v1, /device:TPU:4, one launch (start us, length us, event | category | flops | bytes accessed | tf_op | source)
XLA Modules:
  0.0 2021.9 jit_solution(2429818394373796058)
XLA Ops:
  3.8 110.0 %while.98 = (s32[]{:T(128)}, f32[16,2048]{1,0:T(8,128)S(1)}, bf16[16,16384]{1,0:T(8,128)(2,1)}, s32[1024]{0:T(1024)}, f32[128,1024]{1,0:T(8,128)S(1)}, /*index=5...) while((s32[]{:T(128)}, f32[16,2048]{1,0:T(8,128)S(1)}, ...), condition=%wide.region_1.2_spmd.clone.clone.clone, body=%wide.region_0.1_spmd.clone.clone.clone.sunk | while | flops 184737792 | bytes 51876020 | solution.py:70
  135.5 20.1 fusion.44
  155.6 16.3 broadcast.585.clone
  173.3 315.8 %while.95 = (s32[]{:T(128)}, f32[2,256,768]{2,1,0:T(8,128)}, f32[2,256,768]{2,1,0:T(8,128)}, f32[32,2,256,768]{3,2,1,0:T(8,128)}, f32[32,768]{1,0:T(8,128)}, /*i...) while((s32[]{:T(128)}, f32[2,256,768]{2,1,0:T(8,128)}, ...), condition=%wide.region_3.4_spmd.clone, body=%wide.region_2.3_spmd.clone.sunk | while | flops 5111811 | bytes 33040012 | solution.py:106
  489.1 16.2 broadcast.585.clone.1
  506.7 333.6 %while.96 = (s32[]{:T(128)}, f32[2,256,768]{2,1,0:T(8,128)}, f32[2,256,768]{2,1,0:T(8,128)}, f32[32,2,256,768]{3,2,1,0:T(8,128)}, f32[32,768]{1,0:T(8,128)}, /*i...) while((s32[]{:T(128)}, f32[2,256,768]{2,1,0:T(8,128)}, ...), condition=%wide.region_5.6_spmd.clone, body=%wide.region_4.5_spmd.clone.sunk | while | flops 5505028 | bytes 34612392 | solution.py:117
  840.3 215.6 %while.97 = (s32[]{:T(128)}, f32[2,256,768]{2,1,0:T(8,128)}, f32[2,256,768]{2,1,0:T(8,128)}, f32[2,256,768]{2,1,0:T(8,128)}, f32[2,256,768]{2,1,0:T(8,128)}, /*i...) while((s32[]{:T(128)}, f32[2,256,768]{2,1,0:T(8,128)}, ...), condition=%wide.region_7.8_spmd.clone, body=%wide.region_6.7_spmd.clone.sunk | while | flops 6291459 | bytes 66060612 | solution.py:131
  850.5 10.8 collective-permute-done.1
  881.0 11.7 collective-permute-done.1
  911.2 12.5 collective-permute-done.1
  942.3 12.8 collective-permute-done.1
  973.7 13.1 collective-permute-done.1
  1005.4 13.4 collective-permute-done.1
  1037.4 13.8 collective-permute-done.1
  1055.9 16.3 broadcast.585
  1072.2 114.1 %while.93 = (s32[]{:T(128)}, f32[2,256,768]{2,1,0:T(8,128)}, f32[32,2,256,768]{3,2,1,0:T(8,128)}, f32[32,768]{1,0:T(8,128)}, f32[2,256,768]{2,1,0:T(8,128)S(1)}, /*index=5*/s32[]{:T(128)}) while((s32[]{:T(128)}, f32[2,256,768]{2,1,0:T(8,128)}, f32[32,2,256,768]{3,2,1,0:T(8,128)}, f32[32,768]{1,0:T(8,128)}, f32[2,256,768]{2,1,0:T(8,128)S(1)}, ...), condition=%wide.region_9.10_spmd, body=%wide.region_8.9_spmd.sunk | while | flops 1966082 | bytes 18884196 | solution.py:137
  1195.0 138.6 %while.94 = (s32[]{:T(128)}, f32[2,256,768]{2,1,0:T(8,128)S(1)}, bf16[32,2,256,768]{3,2,1,0:T(8,128)(2,1)}, f32[32,768]{1,0:T(8,128)}, f32[2,256,768]{2,1,0:T(8,...) while((s32[]{:T(128)}, f32[2,256,768]{2,1,0:T(8,128)S(1)}, ...), condition=%wide.region_11.12_spmd, body=%wide.region_10.11_spmd.sunk | while | flops 3538947 | bytes 16524401 | solution.py:144
  1333.6 12.4 slice_bitcast_fusion.3
  1345.9 13.6 pad_maximum_fusion.4
  1359.6 8.8 all-to-all-start.2
  1375.0 535.5 %all-to-all-done.2 = bf16[4,8,2,256,768]{4,3,2,1,0:T(8,128)(2,1)} async-done(((bf16[4,8,2,256,768]{4,3,2,1,0:T(8,128)(2,1)}), bf16[4,8,2,256,768]{4,3,2,1,0:T(8,128)(2,1)}, u32[]{:S(2)}, u32[]{:S(2)}) %all-to-all-start.2) | async-done | bytes 25165856 | tf_op jit(solution)/shard_map/all_to_all | solution.py:158
  1910.5 38.9 %copy.26 = bf16[8,2,4,256,768]{3,2,4,1,0:T(4,128)(2,1)} copy(bf16[8,2,4,256,768]{4,3,1,0,2:T(8,128)(2,1)} %bitcast.14) | data formatting | bytes 50331648 | tf_op jit(solution)/shard_map/reshape | solution.py:157
  1949.4 40.5 %reshape.468 = bf16[8,2,1024,768]{2,3,1,0:T(8,128)(2,1)} reshape(bf16[8,2,4,256,768]{3,2,4,1,0:T(4,128)(2,1)} %copy.26) | data formatting | bytes 50331648 | tf_op jit(solution)/shard_map/reshape | solution.py:157
  1989.9 32.0 %bitcast_convert_fusion = bf16[8,768,1024]{2,1,0:T(8,128)(2,1)} fusion(bf16[8,2,1024,768]{2,3,1,0:T(8,128)(2,1)} %reshape.468, bf16[1,1024,1024]{2,1,0:T(8,128)(2,1)} %get-tuple-element.879, bf16[1,1024,1024]{2,1,0:T(8,128)(2,1)S(1)} %get-tuple-element.878), kind=kOutput, calls=%fused_computation.81 | convolution fusion | flops 25778192384 | bytes 41943040 | tf_op jit(solution)/shard_map/kcfm,cft->kmt/dot_general | solution.py:155
  (1100 shorter events, 1178.6 us)
Async XLA Ops:
  0.0 135.4 %copy-start = (bf16[64,768]{1,0:T(8,128)(2,1)S(1)}, bf16[64,768]{1,0:T(8,128)(2,1)}, u32[]{:S(2)}) copy-start(bf16[64,768]{1,0:T(8,128)(2,1)} %param.22) | copy-start | bytes 294916
  3.8 116.3 %copy-start.16 = (f32[768]{0:T(1024)S(1)}, f32[768]{0:T(1024)}, u32[]{:S(2)}) copy-start(f32[768]{0:T(1024)} %param.25) | copy-start | bytes 9220
  113.8 16.0 copy-start.11
  113.8 16.0 copy-start.13
  113.8 10.3 copy-start.18
  114.4 10.5 all-to-all-start
  124.9 10.5 all-to-all-start.1
  155.6 16.3 copy-start.17
  845.1 16.2 collective-permute-start.1
  848.1 19.0 collective-permute-start
  875.5 17.1 collective-permute-start.1
  878.6 17.5 collective-permute-start
  904.5 19.2 collective-permute-start.1
  909.3 16.9 collective-permute-start
  934.6 20.5 %collective-permute-start.1 = (bf16[2,256,768]{2,1,0:T(8,128)(2,1)}, bf16[2,256,768]{2,1,0:T(8,128)(2,1)}, u32[]{:S(2)}, u32[]{:S(2)}) collective-permute-start(bf16[2,256,768]{2,1,0:T(8,128)(2,1)} %fusion.89), channel_id=1, source_target_pairs={{4,0},{8,4},{12,8},{16,12},{20,16},{24,20},{28,24},{5,1},{9,5},{13... | collective-permute-start | bytes 2359304 | tf_op jit(solution)/shard_map/while/body/eval_jaxpr/ppermute | solution.py:15
  940.4 17.2 collective-permute-start
  965.9 20.9 %collective-permute-start.1 = (bf16[2,256,768]{2,1,0:T(8,128)(2,1)}, bf16[2,256,768]{2,1,0:T(8,128)(2,1)}, u32[]{:S(2)}, u32[]{:S(2)}) collective-permute-start(bf16[2,256,768]{2,1,0:T(8,128)(2,1)} %fusion.89), channel_id=1, source_target_pairs={{4,0},{8,4},{12,8},{16,12},{20,16},{24,20},{28,24},{5,1},{9,5},{13... | collective-permute-start | bytes 2359304 | tf_op jit(solution)/shard_map/while/body/eval_jaxpr/ppermute | solution.py:15
  971.8 17.5 collective-permute-start
  997.6 21.2 %collective-permute-start.1 = (bf16[2,256,768]{2,1,0:T(8,128)(2,1)}, bf16[2,256,768]{2,1,0:T(8,128)(2,1)}, u32[]{:S(2)}, u32[]{:S(2)}) collective-permute-start(bf16[2,256,768]{2,1,0:T(8,128)(2,1)} %fusion.89), channel_id=1, source_target_pairs={{4,0},{8,4},{12,8},{16,12},{20,16},{24,20},{28,24},{5,1},{9,5},{13... | collective-permute-start | bytes 2359304 | tf_op jit(solution)/shard_map/while/body/eval_jaxpr/ppermute | solution.py:15
  1003.4 17.8 collective-permute-start
  1029.6 21.5 %collective-permute-start.1 = (bf16[2,256,768]{2,1,0:T(8,128)(2,1)}, bf16[2,256,768]{2,1,0:T(8,128)(2,1)}, u32[]{:S(2)}, u32[]{:S(2)}) collective-permute-start(bf16[2,256,768]{2,1,0:T(8,128)(2,1)} %fusion.89), channel_id=1, source_target_pairs={{4,0},{8,4},{12,8},{16,12},{20,16},{24,20},{28,24},{5,1},{9,5},{13... | collective-permute-start | bytes 2359304 | tf_op jit(solution)/shard_map/while/body/eval_jaxpr/ppermute | solution.py:15
  1035.4 18.1 collective-permute-start
  1359.6 551.0 %all-to-all-start.2 = ((bf16[4,8,2,256,768]{4,3,2,1,0:T(8,128)(2,1)}), bf16[4,8,2,256,768]{4,3,2,1,0:T(8,128)(2,1)}, u32[]{:S(2)}, u32[]{:S(2)}) async-start(bf16[4,8,2,256,768]{4,3,2,1,0:T(8,128)(2,1)} %pad_maximum_fusion.4), calls=%async_computation.2 | async-start | bytes 50331648 | tf_op jit(solution)/shard_map/all_to_all | solution.py:158
  1989.9 32.0 %copy-start.1 = (bf16[64,768]{1,0:T(8,128)(2,1)S(1)}, bf16[64,768]{1,0:T(8,128)(2,1)}, u32[]{:S(2)}) copy-start(bf16[64,768]{1,0:T(8,128)(2,1)} %param.22) | copy-start | bytes 294916
  (135 other events, 279.7 us)
